TPU v7x, 32 devices: a whole 2x2x4 slice. The times are simulated.
32 devices in a mesh: row: 4 (over z), col: 4 (over x, core), layer: 2 (over y).
Axes of the slice: x: 2, y: 2, z: 4, core: 2. Of those that a mesh axis runs over, the one named last changes fastest.
Arguments:
- intersection: bfloat16 [2048, 2, 1024], P('row', 'layer', 'col'), may hold values from -6 to 6
- density: bfloat16 [2, 1024, 2, 1024], P('layer', 'row', None, 'col'), may hold values from -0.125 to 0.125
- hamiltonian: bfloat16 [2, 1024, 2, 1024], P('layer', 'row', None, 'col'), may hold values from -0.125 to 0.125
- intersection_pattern: int32 [16, 2, 8], P('row', 'layer', 'col'), may hold values 0 or 1
- density_pattern: int32 [2, 8, 2, 8], P('layer', 'row', None, 'col'), may hold values 0 or 1
- hamiltonian_pattern: int32 [2, 8, 2, 8], P('layer', 'row', None, 'col'), may hold values 0 or 1
- product_filter: int32 [16, 2, 8], P('row', 'layer', 'col'), may hold values 0 or 1
Outputs:
- gradient_term: bfloat16 [2048, 2, 1024], P('row', 'layer', 'col')
All inputs are finite; a program needn't handle non-finite values. No bound on the sum of `intersection_pattern` or of `density_pattern` or of `hamiltonian_pattern` or of `product_filter` on one device may be relied on, other than what follows from the above.
Results may differ from a plain program's by a relative error of at most 0.005.
Values may be sent and summed in bfloat16 or wider, within the bound.
No kernel may reach another device: no remote copies, remote signals or barrier semaphores. Data moves between devices by JAX's collectives and lax.ppermute only.
A program may use at most 64 MiB of HBM per device.

v0:
```python
import jax
import jax.numpy as jnp
from jax import lax
from jax.sharding import PartitionSpec as P


def mask_left(block_tile, pattern):
    row_count, _, col_count = block_tile.shape
    row_blocks = pattern.shape[0]
    col_blocks = pattern.shape[2]
    blocks = block_tile.reshape(
        row_blocks, row_count // row_blocks, col_blocks, col_count // col_blocks
    )
    blocks = blocks * pattern.reshape(row_blocks, 1, col_blocks, 1).astype(jnp.bfloat16)
    return blocks.reshape(row_count, col_count)


def mask_right(block_tile, pattern):
    _, row_count, layers, col_count = block_tile.shape
    row_blocks = pattern.shape[1]
    col_blocks = pattern.shape[3]
    blocks = block_tile.reshape(
        row_blocks, row_count // row_blocks, layers, col_blocks, col_count // col_blocks
    )
    blocks = blocks * pattern.reshape(row_blocks, 1, layers, col_blocks, 1).astype(jnp.bfloat16)
    return blocks.reshape(row_count, layers * col_count)


def multiply(left_tile, right_tile):
    whole_left = lax.all_gather(left_tile, "col", axis=1, tiled=True)
    row_count = whole_left.shape[0]
    layers = lax.axis_size("layer")
    column_span = right_tile.shape[1] // layers
    partial_value = jnp.dot(
        whole_left,
        lax.all_gather(right_tile, "row", axis=0, tiled=True),
        preferred_element_type=jnp.float32,
    )
    return lax.psum_scatter(
        partial_value.reshape(row_count, layers, column_span),
        "layer",
        scatter_dimension=1,
        tiled=True,
    )


def local(
    intersection,
    density,
    hamiltonian,
    intersection_pattern,
    density_pattern,
    hamiltonian_pattern,
    product_filter,
):
    left_factor = mask_left(intersection, intersection_pattern)
    right_factor = mask_right(density, density_pattern)
    raw_product = multiply(left_factor, right_factor)
    filtered = mask_left(raw_product.astype(jnp.bfloat16), product_filter)
    masked_ham = mask_right(hamiltonian, hamiltonian_pattern)
    return multiply(filtered, masked_ham).astype(jnp.bfloat16)


def solution(mesh):
    placed = (
        P("row", "layer", "col"),
        P("layer", "row", None, "col"),
        P("layer", "row", None, "col"),
        P("row", "layer", "col"),
        P("layer", "row", None, "col"),
        P("layer", "row", None, "col"),
        P("row", "layer", "col"),
    )
    return jax.shard_map(
        local, mesh=mesh, in_specs=placed, out_specs=P("row", "layer", "col"), check_vma=False
    )
```

profile of v0, /device:TPU:0, one launch (start us, length us, event | category | flops | bytes accessed | tf_op | source)
XLA Modules:
  0.0 161.6 jit_solution(11556054652740069047)
XLA Ops:
  6.5 0.7 convert_bitcast_fusion.1
  7.2 0.2 mul.47
  7.4 0.1 mul.48
  7.6 0.8 copy-done.1
  8.4 0.8 mul.49
  9.2 0.0 all-gather.5.cloned.1.call-start
  9.3 0.1 copy.8
  9.4 0.2 mul.44
  9.6 0.5 copy-done
  10.2 0.7 bitcast_multiply_fusion.1
  10.9 0.0 reduce-scatter.3.cloned.1.call-start
  11.0 29.0 %all-gather.7.cloned.1.call-done = bf16[1024,512]{1,0:T(8,128)(2,1)} async-done(((bf16[256,512]{1,0:T(8,128)(2,1)}), bf16[1024,512]{1,0:T(8,128)(2,1)}) %all-gather.7.cloned.1.call-update) | async-done | bytes 1048592 | tf_op jit(solution)/shard_map/all_gather | solution.py:36
  40.0 17.9 %all-gather.5.cloned.1.call-done = bf16[512,1024]{1,0:T(8,128)(2,1)} async-done(((bf16[512,256]{1,0:T(8,128)(2,1)}), bf16[512,1024]{1,0:T(8,128)(2,1)}) %all-gather.5.cloned.1.call-update) | async-done | bytes 1048592 | tf_op jit(solution)/shard_map/all_gather | solution.py:30
  57.9 3.3 %fusion = f32[512,512]{0,1:T(8,128)} fusion(bf16[512,1024]{1,0:T(8,128)(2,1)} %all-gather.5.cloned.1.call-done, bf16[1024,512]{1,0:T(8,128)(2,1)} %all-gather.7.cloned.1.call-done), kind=kOutput, calls=%fused_computation.6 | convolution fusion | flops 536870912 | bytes 3145728 | tf_op jit(solution)/shard_map/dot_general | solution.py:34
  61.2 0.0 all-gather.11.cloned.1.call-start
  61.3 0.6 copy-done.3
  61.9 0.2 mul.53
  62.1 0.1 mul.54
  62.2 0.8 copy-done.2
  63.1 0.8 mul.55
  63.9 0.0 all-gather.9.cloned.1.call-start
  64.0 0.6 copy-done.5
  64.6 17.1 %reduce-scatter.3.cloned.1.call-done = f32[512,1,256]{0,2,1:T(8,128)} async-done(((f32[512,2,256]{0,2,1:T(8,128)}), f32[512,1,256]{0,2,1:T(8,128)}) %reduce-scatter.3.cloned.1.call-update) | async-done | bytes 524304 | tf_op jit(solution)/shard_map/reduce_scatter | solution.py:39
  81.7 0.1 mul.50
  81.9 1.8 %bitcast_multiply_fusion = bf16[512,256]{0,1:T(8,128)(2,1)} fusion(bf16[32,8,4,128]{3,2,1,0:T(4,128)(2,1)S(1)} %bitcast.39, f32[512,1,256]{0,2,1:T(8,128)} %reduce-scatter.3.cloned.1.call-done), kind=kLoop, calls=%fused_computation | loop fusion | flops 262144 | bytes 1048576 | tf_op jit(solution)/shard_map/mul | solution.py:14
  83.7 0.0 reduce-scatter.5.cloned.1.call-start
  83.7 27.4 %all-gather.11.cloned.1.call-done = bf16[1024,512]{1,0:T(8,128)(2,1)} async-done(((bf16[256,512]{1,0:T(8,128)(2,1)}), bf16[1024,512]{1,0:T(8,128)(2,1)}) %all-gather.11.cloned.1.call-update) | async-done | bytes 1048592 | tf_op jit(solution)/shard_map/all_gather | solution.py:36
  111.2 17.7 %all-gather.9.cloned.1.call-done = bf16[512,1024]{0,1:T(8,128)(2,1)} async-done(((bf16[512,256]{0,1:T(8,128)(2,1)}), bf16[512,1024]{0,1:T(8,128)(2,1)}) %all-gather.9.cloned.1.call-update) | async-done | bytes 1048592 | tf_op jit(solution)/shard_map/all_gather | solution.py:30
  128.9 2.3 %fusion.1 = f32[512,512]{0,1:T(8,128)S(1)} fusion(bf16[512,1024]{0,1:T(8,128)(2,1)} %all-gather.9.cloned.1.call-done, bf16[1024,512]{1,0:T(8,128)(2,1)} %all-gather.11.cloned.1.call-done), kind=kOutput, calls=%fused_computation.7 | convolution fusion | flops 536870912 | bytes 3145728 | tf_op jit(solution)/shard_map/dot_general | solution.py:34
  131.2 1.3 copy.9
  132.5 20.5 %reduce-scatter.5.cloned.1.call-done = f32[512,1,256]{2,0,1:T(8,128)} async-done(((f32[512,2,256]{2,0,1:T(8,128)}), f32[512,1,256]{2,0,1:T(8,128)}) %reduce-scatter.5.cloned.1.call-update) | async-done | bytes 524304 | tf_op jit(solution)/shard_map/reduce_scatter | solution.py:39
  153.0 1.8 %convert_element_type.59 = bf16[512,1,256]{2,0,1:T(8,128)(2,1)} convert(f32[512,1,256]{2,0,1:T(8,128)} %reduce-scatter.5.cloned.1.call-done) | non-fusion elementwise | flops 131072 | bytes 786432 | tf_op jit(solution)/shard_map/convert_element_type | solution.py:61
  (19 shorter events, 0.2 us)
Async XLA Ops:
  6.5 33.5 %all-gather.7.cloned.1.call-start = ((), (), s32[]{:S(2)}) async-start(), calls=%async_computation.3 | async-start | bytes 1310720 | tf_op jit(solution)/shard_map/all_gather | solution.py:36
  7.4 1.0 copy-start.1
  8.4 0.9 copy-start.4
  9.2 0.9 copy-start
  9.2 48.7 %all-gather.5.cloned.1.call-start = ((), (), s32[]{:S(2)}) async-start(), calls=%async_computation.2 | async-start | bytes 1310720 | tf_op jit(solution)/shard_map/all_gather | solution.py:30
  10.9 70.8 %reduce-scatter.3.cloned.1.call-start = ((), (), s32[]{:S(2)}) async-start(), calls=%async_computation.4 | async-start | bytes 1572864 | tf_op jit(solution)/shard_map/reduce_scatter | solution.py:39
  61.2 0.7 copy-start.3
  61.2 49.9 %all-gather.11.cloned.1.call-start = ((), (), s32[]{:S(2)}) async-start(), calls=%async_computation.6 | async-start | bytes 1310720 | tf_op jit(solution)/shard_map/all_gather | solution.py:36
  62.1 1.0 copy-start.2
  63.9 0.7 copy-start.5
  63.9 65.0 %all-gather.9.cloned.1.call-start = ((), (), s32[]{:S(2)}) async-start(), calls=%async_computation.5 | async-start | bytes 1310720 | tf_op jit(solution)/shard_map/all_gather | solution.py:30
  83.7 69.3 %reduce-scatter.5.cloned.1.call-start = ((), (), s32[]{:S(2)}) async-start(), calls=%async_computation.7 | async-start | bytes 1572864 | tf_op jit(solution)/shard_map/reduce_scatter | solution.py:39
Sparse Core Ops, SparseCore 0:
  9.4 30.6 all-gather.6
  41.6 16.3 all-gather.4
  61.4 20.3 reduce-scatter.2
  83.2 27.9 all-gather.10
  112.7 16.2 all-gather.8
  132.7 20.3 reduce-scatter.4
where the time goes:
time: 162 us
  waiting for transfers between devices  130 us (80%)
  between operations  13.6 us (8%)
  other arithmetic  6.58 us (4%)
  local copies, waits for them, and re-layouts  5.88 us (4%)
  matrix products  5.57 us (3%)
    all_gather x2, waiting for transfers between devices, multiply(): lax.all_gather(right_tile, 'row', axis=0, tiled=True)  56.5 us
    reduce_scatter x2, waiting for transfers between devices, multiply(): lax.psum_scatter(partial_value.reshape(row_count, layers, column_span), '...  37.6 us
    all_gather x2, waiting for transfers between devices, multiply(): whole_left = lax.all_gather(left_tile, 'col', axis=1, tiled=True)  35.6 us
    dot_general x2, matrix products, multiply(): jnp.dot(whole_left, lax.all_gather(right_tile, 'row', axis=0, tiled=True)...  5.57 us
    unnamed x14, local copies, waits for them, and re-layouts  3.49 us
  transfers between devices with their start and end apart: 6, of which 6 were waited for; matrix products, arithmetic and copies ran while one was open for 3% of the time, Pallas kernels for 0%

commit v1 on v0

--- a/solution.py
+++ b/solution.py
@@ -27,7 +27,12 @@
 
 
 def multiply(left_tile, right_tile):
-    whole_left = lax.all_gather(left_tile, "col", axis=1, tiled=True)
+    ring = [left_tile]
+    for hop in range(3):
+        ring.append(lax.ppermute(ring[-1], "col", [(dev, (dev + 1) % 4) for dev in range(4)]))
+    whole_left = jnp.roll(
+        jnp.concatenate(ring[::-1], axis=1), (lax.axis_index("col") + 1) * ring[0].shape[1], axis=1
+    )
     row_count = whole_left.shape[0]
     layers = lax.axis_size("layer")
     column_span = right_tile.shape[1] // layers

time: 162 us -> 129 us (0.80)
  waiting for transfers between devices: 130 us -> 96.2 us
  matrix products: 5.57 us -> 9.07 us
  local copies, waits for them, and re-layouts: 5.88 us -> 4.08 us
    all_gather x2 -> x0, waiting for transfers between devices: 35.6 us -> none  [multiply(): whole_left = lax.all_gather(left_tile, 'col', axis=1, tiled=True)]
    ppermute x0 -> x6, waiting for transfers between devices: none -> 29.2 us  [multiply(): lax.ppermute(ring[-1], 'col', [(dev, (dev + 1) % 4) for dev in range(4)])]
    all_gather x2, waiting for transfers between devices: 56.5 us -> 29 us  [multiply(): lax.all_gather(right_tile, 'row', axis=0, tiled=True)]
    dot_general x2, matrix products: 5.57 us -> 9.07 us  [multiply(): jnp.dot(whole_left, lax.all_gather(right_tile, 'row', axis=0, tiled=True)...]
    unnamed x14 -> x12, local copies, waits for them, and re-layouts: 3.49 us -> 1.68 us
  transfers between devices with their start and end apart: 6 -> 10, of which waited for: 6 -> 9; matrix products, arithmetic and copies ran while one was open for 3% -> 2% of each run, Pallas kernels for 0% -> 0%
where the time goes in v1:
time: 129 us; the launch traced here: 128 us
  waiting for transfers between devices  96.2 us (75%)
  between operations  13.3 us (10%)
  matrix products  9.07 us (7%)
  other arithmetic  5.16 us (4%)
  local copies, waits for them, and re-layouts  4.08 us (3%)
    reduce_scatter x2, waiting for transfers between devices, multiply(): lax.psum_scatter(partial_value.reshape(row_count, layers, column_span), '...  38 us
    ppermute x6, waiting for transfers between devices, multiply(): lax.ppermute(ring[-1], 'col', [(dev, (dev + 1) % 4) for dev in range(4)])  29.2 us
    all_gather x2, waiting for transfers between devices, multiply(): lax.all_gather(right_tile, 'row', axis=0, tiled=True)  29 us
    dot_general x2, matrix products, multiply(): jnp.dot(whole_left, lax.all_gather(right_tile, 'row', axis=0, tiled=True)...  9.07 us
  transfers between devices with their start and end apart: 10, of which 9 were waited for; matrix products, arithmetic and copies ran while one was open for 2% of the time, Pallas kernels for 0%

profile of v1, /device:TPU:0, one launch (start us, length us, event | category | flops | bytes accessed | tf_op | source)
XLA Modules:
  0.0 128.5 jit_solution(15443183676825115928)
XLA Ops:
  6.5 0.7 convert_bitcast_fusion.1
  7.2 0.2 mul.52
  7.4 0.1 mul.53
  7.6 1.0 copy.11
  8.6 0.8 mul.54
  9.4 0.0 all-gather.3.cloned.1.call-update
  9.4 0.0 reduce-scatter.3.cloned.1.call-start
  9.5 0.1 copy.8
  9.6 0.2 mul.48
  9.8 0.5 collective-permute-start
  10.3 6.0 %collective-permute-done = bf16[512,256]{1,0:T(8,128)(2,1)S(1)} collective-permute-done((bf16[512,256]{1,0:T(8,128)(2,1)S(1)}, bf16[512,256]{1,0:T(8,128)(2,1)S(1)}, u32[]{:S(2)}, u32[]{:S(2)}) %collective-permute-start) | collective-permute-done | bytes 262176 | tf_op jit(solution)/shard_map/ppermute | solution.py:32
  16.3 5.8 %collective-permute-done.1 = bf16[512,256]{1,0:T(8,128)(2,1)S(1)} collective-permute-done((bf16[512,256]{1,0:T(8,128)(2,1)S(1)}, bf16[512,256]{1,0:T(8,128)(2,1)S(1)}, u32[]{:S(2)}, u32[]{:S(2)}) %collective-permute-start.1) | collective-permute-done | bytes 262176 | tf_op jit(solution)/shard_map/ppermute | solution.py:32
  22.1 5.8 %collective-permute-done.2 = bf16[512,256]{1,0:T(8,128)(2,1)S(1)} collective-permute-done((bf16[512,256]{1,0:T(8,128)(2,1)S(1)}, bf16[512,256]{1,0:T(8,128)(2,1)S(1)}, u32[]{:S(2)}, u32[]{:S(2)}) %collective-permute-start.2) | collective-permute-done | bytes 262176 | tf_op jit(solution)/shard_map/ppermute | solution.py:32
  27.9 12.3 %all-gather.3.cloned.1.call-done = bf16[1024,512]{1,0:T(8,128)(2,1)} async-done(((bf16[256,512]{1,0:T(8,128)(2,1)}), bf16[1024,512]{1,0:T(8,128)(2,1)}) %all-gather.3.cloned.1.call-update) | async-done | bytes 1048592 | tf_op jit(solution)/shard_map/all_gather | solution.py:41
  40.2 4.1 %fusion.14 = f32[512,512]{0,1:T(8,128)} fusion(bf16[1024,512]{1,0:T(8,128)(2,1)} %all-gather.3.cloned.1.call-done, s32[]{:T(128)S(6)} %select_n.13, bf16[512,256]{1,0:T(8,128)(2,1)S(1)} %collective-permute-done.2, bf16[512,256]{1,0:T(8,128)(2,1)S(1)} %collective-permute-done.1, bf16[512,256]{1,0:T(8,128)(2,1)S(1)} %collective-permute-done, ...), kind=kOutput, calls=%fused_computation.28 | convolution fusion | flops 545259520 | bytes 3145732 | tf_op jit(solution)/shard_map/dot_general | solution.py:39
  44.3 0.0 all-gather.5.cloned.1.call-start
  44.3 0.6 copy-done.2
  44.9 0.2 mul.58
  45.1 0.1 mul.59
  45.3 0.8 mul.60
  46.1 0.0 reduce-scatter.5.cloned.1.call-start
  46.2 18.0 %reduce-scatter.3.cloned.1.call-done = f32[512,1,256]{0,2,1:T(8,128)} async-done(((f32[512,2,256]{0,2,1:T(8,128)}), f32[512,1,256]{0,2,1:T(8,128)}) %reduce-scatter.3.cloned.1.call-update) | async-done | bytes 524304 | tf_op jit(solution)/shard_map/reduce_scatter | solution.py:44
  64.2 0.1 mul.55
  64.3 1.1 bitcast_multiply_fusion
  65.5 0.1 collective-permute-start.3
  65.5 5.8 %collective-permute-done.3 = bf16[512,256]{0,1:T(8,128)(2,1)S(1)} collective-permute-done((bf16[512,256]{0,1:T(8,128)(2,1)S(1)}, bf16[512,256]{0,1:T(8,128)(2,1)S(1)}, u32[]{:S(2)}, u32[]{:S(2)}) %collective-permute-start.3) | collective-permute-done | bytes 262176 | tf_op jit(solution)/shard_map/ppermute | solution.py:32
  71.3 5.8 %collective-permute-done.4 = bf16[512,256]{0,1:T(8,128)(2,1)S(1)} collective-permute-done((bf16[512,256]{0,1:T(8,128)(2,1)S(1)}, bf16[512,256]{0,1:T(8,128)(2,1)S(1)}, u32[]{:S(2)}, u32[]{:S(2)}) %collective-permute-start.4) | collective-permute-done | bytes 262176 | tf_op jit(solution)/shard_map/ppermute | solution.py:32
  77.1 16.7 %all-gather.5.cloned.1.call-done = bf16[1024,512]{1,0:T(8,128)(2,1)} async-done(((bf16[256,512]{1,0:T(8,128)(2,1)}), bf16[1024,512]{1,0:T(8,128)(2,1)}) %all-gather.5.cloned.1.call-update) | async-done | bytes 1048592 | tf_op jit(solution)/shard_map/all_gather | solution.py:41
  93.8 5.0 %fusion.4 = f32[512,512]{0,1:T(8,128)S(1)} fusion(bf16[1024,512]{1,0:T(8,128)(2,1)} %all-gather.5.cloned.1.call-done, s32[]{:T(128)S(6)} %select_n.13, bf16[512,256]{0,1:T(8,128)(2,1)S(1)} %collective-permute-done.5, bf16[512,256]{0,1:T(8,128)(2,1)S(1)} %collective-permute-done.4, bf16[512,256]{0,1:T(8,128)(2,1)S(1)} %collective-permute-done.3, ...), kind=kOutput, calls=%fused_computation.20 | convolution fusion | flops 545259520 | bytes 3145732 | tf_op jit(solution)/shard_map/dot_general | solution.py:39
  98.9 1.3 %copy.9 = f32[512,2,256]{2,0,1:T(8,128)} copy(f32[512,2,256]{0,2,1:T(8,128)S(1)} %bitcast.36) | data formatting | bytes 2097152 | tf_op jit(solution)/shard_map/reshape | solution.py:45
  100.2 20.0 %reduce-scatter.5.cloned.1.call-done = f32[512,1,256]{2,0,1:T(8,128)} async-done(((f32[512,2,256]{2,0,1:T(8,128)}), f32[512,1,256]{2,0,1:T(8,128)}) %reduce-scatter.5.cloned.1.call-update) | async-done | bytes 524304 | tf_op jit(solution)/shard_map/reduce_scatter | solution.py:44
  120.2 1.8 %convert_element_type.59 = bf16[512,1,256]{2,0,1:T(8,128)(2,1)} convert(f32[512,1,256]{2,0,1:T(8,128)} %reduce-scatter.5.cloned.1.call-done) | non-fusion elementwise | flops 131072 | bytes 786432 | tf_op jit(solution)/shard_map/convert_element_type | solution.py:66
  (23 shorter events, 0.2 us)
Async XLA Ops:
  6.5 33.6 %all-gather.3.cloned.1.call-start = ((), (), s32[]{:S(2)}) async-start(), calls=%async_computation.2 | async-start | bytes 1310720 | tf_op jit(solution)/shard_map/all_gather | solution.py:41
  7.4 2.0 %copy-start.3 = (s32[4,1,2]{0,2,1:T(2,128)S(1)}, s32[4,1,2]{0,2,1:T(2,128)}, u32[]{:S(2)}) copy-start(s32[4,1,2]{0,2,1:T(2,128)} %param.12) | copy-start | bytes 100
  7.6 2.2 %copy-start = (bf16[512,1,256]{2,0,1:T(8,128)(2,1)S(1)}, bf16[512,1,256]{2,0,1:T(8,128)(2,1)}, u32[]{:S(2)}) copy-start(bf16[512,1,256]{2,0,1:T(8,128)(2,1)} %param.9) | copy-start | bytes 786436
  9.4 54.8 %reduce-scatter.3.cloned.1.call-start = ((), (), s32[]{:S(2)}) async-start(), calls=%async_computation.3 | async-start | bytes 1572864 | tf_op jit(solution)/shard_map/reduce_scatter | solution.py:44
  9.8 6.5 %collective-permute-start = (bf16[512,256]{1,0:T(8,128)(2,1)S(1)}, bf16[512,256]{1,0:T(8,128)(2,1)S(1)}, u32[]{:S(2)}, u32[]{:S(2)}) collective-permute-start(bf16[512,256]{1,0:T(8,128)(2,1)S(1)} %bitcast_multiply_fusion.1), channel_id=1, source_target_pairs={{0,2},{2,4},{4,6},{6,0},{1,3},{3,5},{5,7},{7,1},{8,10},{10,12},{12... | collective-permute-start | bytes 786440 | tf_op jit(solution)/shard_map/ppermute | solution.py:32
  16.3 5.8 %collective-permute-start.1 = (bf16[512,256]{1,0:T(8,128)(2,1)S(1)}, bf16[512,256]{1,0:T(8,128)(2,1)S(1)}, u32[]{:S(2)}, u32[]{:S(2)}) collective-permute-start(bf16[512,256]{1,0:T(8,128)(2,1)S(1)} %collective-permute-done), channel_id=1, source_target_pairs={{0,2},{2,4},{4,6},{6,0},{1,3},{3,5},{5,7},{7,1},{8,10},{10,12},{12... | collective-permute-start | bytes 786440 | tf_op jit(solution)/shard_map/ppermute | solution.py:32
  22.1 5.8 %collective-permute-start.2 = (bf16[512,256]{1,0:T(8,128)(2,1)S(1)}, bf16[512,256]{1,0:T(8,128)(2,1)S(1)}, u32[]{:S(2)}, u32[]{:S(2)}) collective-permute-start(bf16[512,256]{1,0:T(8,128)(2,1)S(1)} %collective-permute-done.1), channel_id=1, source_target_pairs={{0,2},{2,4},{4,6},{6,0},{1,3},{3,5},{5,7},{7,1},{8,10},{10,12},{12... | collective-permute-start | bytes 786440 | tf_op jit(solution)/shard_map/ppermute | solution.py:32
  44.2 0.7 copy-start.2
  44.2 1.0 copy-start.1
  44.3 49.6 %all-gather.5.cloned.1.call-start = ((), (), s32[]{:S(2)}) async-start(), calls=%async_computation.4 | async-start | bytes 1310720 | tf_op jit(solution)/shard_map/all_gather | solution.py:41
  45.1 1.0 copy-start.4
  46.1 74.1 %reduce-scatter.5.cloned.1.call-start = ((), (), s32[]{:S(2)}) async-start(), calls=%async_computation.5 | async-start | bytes 1572864 | tf_op jit(solution)/shard_map/reduce_scatter | solution.py:44
  65.5 5.8 %collective-permute-start.3 = (bf16[512,256]{0,1:T(8,128)(2,1)S(1)}, bf16[512,256]{0,1:T(8,128)(2,1)S(1)}, u32[]{:S(2)}, u32[]{:S(2)}) collective-permute-start(bf16[512,256]{0,1:T(8,128)(2,1)S(1)} %bitcast_multiply_fusion), channel_id=1, source_target_pairs={{0,2},{2,4},{4,6},{6,0},{1,3},{3,5},{5,7},{7,1},{8,10},{10,12},{12... | collective-permute-start | bytes 786440 | tf_op jit(solution)/shard_map/ppermute | solution.py:32
  71.3 5.8 %collective-permute-start.4 = (bf16[512,256]{0,1:T(8,128)(2,1)S(1)}, bf16[512,256]{0,1:T(8,128)(2,1)S(1)}, u32[]{:S(2)}, u32[]{:S(2)}) collective-permute-start(bf16[512,256]{0,1:T(8,128)(2,1)S(1)} %collective-permute-done.3), channel_id=1, source_target_pairs={{0,2},{2,4},{4,6},{6,0},{1,3},{3,5},{5,7},{7,1},{8,10},{10,12},{12... | collective-permute-start | bytes 786440 | tf_op jit(solution)/shard_map/ppermute | solution.py:32
  77.1 16.7 %collective-permute-start.5 = (bf16[512,256]{0,1:T(8,128)(2,1)S(1)}, bf16[512,256]{0,1:T(8,128)(2,1)S(1)}, u32[]{:S(2)}, u32[]{:S(2)}) collective-permute-start(bf16[512,256]{0,1:T(8,128)(2,1)S(1)} %collective-permute-done.4), channel_id=1, source_target_pairs={{0,2},{2,4},{4,6},{6,0},{1,3},{3,5},{5,7},{7,1},{8,10},{10,12},{12... | collective-permute-start | bytes 786440 | tf_op jit(solution)/shard_map/ppermute | solution.py:32
Sparse Core Ops, SparseCore 0:
  9.5 30.6 all-gather.2
  44.4 19.7 reduce-scatter.2
  65.9 27.9 all-gather.4
  100.3 19.7 reduce-scatter.4
